TPU v7x, 256 devices: a whole 4x4x8 slice. The times are simulated.
256 devices in a mesh: ta: 4 (over z_lo, core), pa: 64 (over x, y, z_hi).
Axes of the slice: x: 4, y: 4, z: 8 (z_hi: 4, z_lo: 2; z = z_hi * 2 + z_lo), core: 2. Of those that a mesh axis runs over, the one named last changes fastest.
Arguments:
- green_freq: bfloat16 [256, 4, 256, 256], P('ta', None, 'pa'), may hold values from -6 to 6
- colloc: bfloat16 [4, 256, 1024], P(None, None, 'pa'), may hold values from -0.375 to 0.375
- core: bfloat16 [1024, 1024], replicated, may hold values from -0.1875 to 0.1875
Outputs:
- sigma_freq: bfloat16 [256, 4, 256, 256], P('ta', None, 'pa')
All inputs are finite; a program needn't handle non-finite values.
Results may differ from a plain program's by a relative error of at most 0.03.
Values may be sent and summed in bfloat16 or wider, within the bound.
No kernel may reach another device: no remote copies, remote signals or barrier semaphores. Data moves between devices by JAX's collectives and lax.ppermute only.
A program may use at most 128 MiB of HBM per device.

v0:
```python
import jax
import jax.numpy as jnp
from jax import lax
from jax.sharding import PartitionSpec as P

NFREQ = 128
NTIME = 128


def cut_along(array, dim, length):
    lengths = array.shape
    blocks = array.reshape(*lengths[:dim], length, lengths[dim] // length, *lengths[dim + 1 :])
    return jnp.moveaxis(blocks, dim, 0)


def summed_on_arrival(array, axis, dim):
    blocks = cut_along(array, dim, lax.axis_size(axis))
    arrived = lax.all_to_all(blocks, axis, split_axis=0, concat_axis=0, tiled=True)
    return arrived.astype(jnp.float32).sum(axis=0)


def time_tables(nfreq, ntime):
    freq = jnp.arange(nfreq, dtype=jnp.float32)
    times = jnp.arange(ntime, dtype=jnp.float32)
    phase = jnp.pi * (2.0 * freq[None, :] + 1.0) * (times[:, None] + 0.5) / ntime
    cosine = jnp.cos(phase)
    sine = jnp.sin(phase)
    scale_fwd = 1.0 / jnp.sqrt(jnp.float32(nfreq))
    scale_back = 1.0 / jnp.sqrt(jnp.float32(ntime))
    plus = jnp.concatenate([cosine, sine], axis=1) * scale_fwd
    minus = jnp.concatenate([-cosine, sine], axis=1) * scale_fwd
    fwd = jnp.stack([plus, minus], axis=0)
    back = jnp.concatenate([cosine.T, sine.T], axis=0) * scale_back
    return (fwd, back)


def local(green_freq, colloc, core):
    fwd, back = time_tables(NFREQ, NTIME)
    freq_rows = green_freq.shape[0]
    first = lax.axis_index("ta") * freq_rows
    fwd_part = lax.dynamic_slice_in_dim(fwd, first, freq_rows, 2)
    partial_time = jnp.einsum(
        "stw,wkij->stkij", fwd_part, green_freq.astype(jnp.float32), precision=lax.Precision.HIGHEST
    )
    green_time = summed_on_arrival(partial_time.astype(jnp.bfloat16), "ta", 1).astype(jnp.bfloat16)
    piece = lax.all_gather(colloc, "pa", axis=2, tiled=True)
    half_piece = jnp.einsum(
        "stkij,kjq->stkiq", green_time, piece, preferred_element_type=jnp.float32
    ).astype(jnp.bfloat16)
    gathered = piece[None, None]
    full_colloc = gathered[0, 0]
    kcount = full_colloc.shape[0]
    green_pts = jnp.einsum(
        "kip,stkiq->stkpq",
        full_colloc,
        lax.all_to_all(half_piece, "pa", split_axis=4, concat_axis=3, tiled=True),
        preferred_element_type=jnp.float32,
    )
    bubble_block = (jnp.sum(green_pts[0] * green_pts[1], axis=1) / kcount).astype(jnp.bfloat16)
    green_plus = green_pts[0]
    mixed = jnp.einsum(
        "pr,trq->tpq", core, bubble_block, preferred_element_type=jnp.float32
    ).astype(jnp.bfloat16)
    mixed_rows = lax.all_to_all(mixed, "pa", split_axis=1, concat_axis=2, tiled=True)
    screened_rows = jnp.einsum(
        "tps,sq->tpq", mixed_rows, core, preferred_element_type=jnp.float32
    ).astype(jnp.bfloat16)
    screened = lax.all_to_all(screened_rows, "pa", split_axis=2, concat_axis=1, tiled=True)
    source = (-green_plus * screened.astype(jnp.float32)[:, None]).astype(jnp.bfloat16)
    outer = jnp.einsum(
        "kip,tkpq->tkiq", full_colloc, source, preferred_element_type=jnp.float32
    ).astype(jnp.bfloat16)
    sigma_time = jnp.einsum(
        "tkiq,kjq->tkij",
        lax.all_to_all(outer, "pa", split_axis=2, concat_axis=3, tiled=True),
        full_colloc,
        preferred_element_type=jnp.float32,
    ).astype(jnp.bfloat16)
    time_rows = sigma_time.shape[0]
    first_time = lax.axis_index("ta") * time_rows
    back_part = lax.dynamic_slice_in_dim(back, first_time, time_rows, 1)
    partial_freq = jnp.einsum(
        "wt,tkij->wkij", back_part, sigma_time.astype(jnp.float32), precision=lax.Precision.HIGHEST
    )
    return summed_on_arrival(partial_freq.astype(jnp.bfloat16), "ta", 0).astype(jnp.bfloat16)


def solution(mesh):
    return jax.shard_map(
        local,
        mesh=mesh,
        in_specs=(P("ta", None, "pa", None), P(None, None, "pa"), P()),
        out_specs=P("ta", None, "pa", None),
        check_vma=False,
    )
```

profile of v0, /device:TPU:1, one launch (start us, length us, event | category | flops | bytes accessed | tf_op | source)
XLA Modules:
  0.0 482.5 jit_solution(289619318880138585)
XLA Ops:
  11.0 31.8 %all_to_all.73 = bf16[4,2,32,4,4,256]{5,2,4,3,1,0:T(8,128)(2,1)} all-to-all(bf16[4,2,32,4,4,256]{5,2,4,3,1,0:T(8,128)(2,1)S(1)} %bitcast.122), channel_id=1, replica_groups=mesh['ta'=4,'pa'=64] {'ta'}, dimensions={0} | all-to-all | bytes 4194304 | tf_op jit(solution)/shard_map/all_to_all | solution.py:18
  44.8 48.7 %all-gather.2.cloned.1.call-done = bf16[4,256,1024]{1,2,0:T(8,128)(2,1)} async-done(((bf16[4,256,16]{1,2,0:T(8,128)(2,1)}), bf16[4,256,1024]{1,2,0:T(8,128)(2,1)}) %all-gather.2.cloned.1.call-update) | async-done | bytes 2097168 | tf_op jit(solution)/shard_map/all_gather | solution.py:46
  93.5 3.7 convert_bitcast_fusion
  97.1 13.3 %copy.69 = bf16[2,32,4,4,1024]{1,3,0,2,4:T(4,128)(2,1)} copy(bf16[2,32,4,4,1024]{4,1,3,0,2:T(8,128)(2,1)} %convert_bitcast_fusion) | data formatting | bytes 4194304 | tf_op jit(solution)/shard_map/convert_element_type | solution.py:49
  110.4 13.7 %reshape.210 = bf16[64,2,8192]{2,1,0:T(2,128)(2,1)} reshape(bf16[1024,4,2,4,32]{4,3,2,1,0:T(4,128)(2,1)} %bitcast.106) | data formatting | bytes 4194304
  124.1 63.4 %all_to_all.74 = bf16[64,2,8192]{2,1,0:T(2,128)(2,1)} all-to-all(bf16[64,2,8192]{2,1,0:T(2,128)(2,1)} %reshape.210), channel_id=1, replica_groups=mesh['ta'=4,'pa'=64] {'pa'}, dimensions={0} | all-to-all | bytes 4194304 | tf_op jit(solution)/shard_map/all_to_all | solution.py:56
  187.5 13.3 %reshape.211 = bf16[1024,4,2,4,32]{4,3,2,1,0:T(4,128)(2,1)} reshape(bf16[64,2,8192]{2,1,0:T(2,128)(2,1)} %all_to_all.74) | data formatting | bytes 4194304
  200.8 9.8 %copy.70 = bf16[2,32,4,4,1024]{1,4,3,2,0:T(8,128)(2,1)} copy(bf16[2,32,4,4,1024]{1,3,0,2,4:T(4,128)(2,1)} %bitcast.107) | data formatting | bytes 4194304 | tf_op jit(solution)/shard_map/all_to_all | solution.py:56
  210.6 9.1 %copy.71 = bf16[2,32,4,64,4,16]{1,5,4,3,2,0:T(8,128)(2,1)} copy(bf16[2,32,4,64,4,16]{1,5,3,4,2,0:T(8,128)(2,1)} %bitcast.110) | data formatting | bytes 4194304 | tf_op jit(solution)/shard_map/all_to_all | solution.py:56
  219.7 11.9 %copy.72 = bf16[2,32,4,256,16]{3,4,1,0,2:T(8,128)(2,1)} copy(bf16[2,32,4,256,16]{1,4,3,2,0:T(8,128)(2,1)} %bitcast.108) | data formatting | bytes 4194304 | tf_op jit(solution)/shard_map/all_to_all | solution.py:56
  231.6 4.6 convolution_bitcast_fusion
  243.4 5.1 %copy.73 = bf16[32,1024,16]{0,2,1:T(8,128)(2,1)} copy(bf16[32,1024,16]{1,2,0:T(8,128)(2,1)S(1)} %fusion.28) | data formatting | bytes 2097152 | tf_op jit(solution)/shard_map/convert_element_type | solution.py:63
  248.5 6.4 %reshape.212 = bf16[64,2,4096]{2,1,0:T(2,128)(2,1)S(1)} reshape(bf16[1024,16,32]{2,1,0:T(8,128)(2,1)} %bitcast.113) | data formatting | bytes 2097152
  255.0 33.4 %all_to_all.75 = bf16[64,2,4096]{2,1,0:T(2,128)(2,1)} all-to-all(bf16[64,2,4096]{2,1,0:T(2,128)(2,1)S(1)} %reshape.212), channel_id=1, replica_groups=mesh['ta'=4,'pa'=64] {'pa'}, dimensions={0} | all-to-all | bytes 2097152 | tf_op jit(solution)/shard_map/all_to_all | solution.py:64
  288.4 6.5 %reshape.213 = bf16[1024,16,32]{2,1,0:T(8,128)(2,1)} reshape(bf16[64,2,4096]{2,1,0:T(2,128)(2,1)} %all_to_all.75) | data formatting | bytes 2097152
  294.9 5.2 %copy.74 = bf16[32,16,64,16]{0,3,2,1:T(8,128)(2,1)} copy(bf16[32,16,64,16]{0,3,1,2:T(8,128)(2,1)} %bitcast.117) | data formatting | bytes 2097152 | tf_op jit(solution)/shard_map/all_to_all | solution.py:64
  300.1 4.0 copy.75
  306.3 7.4 %copy.76 = bf16[32,16,1024]{0,1,2:T(8,128)(2,1)} copy(bf16[32,16,1024]{2,1,0:T(8,128)(2,1)} %fusion.25) | data formatting | bytes 2097152 | tf_op jit(solution)/shard_map/convert_element_type | solution.py:67
  313.7 6.4 %reshape.214 = bf16[64,2,4096]{2,1,0:T(2,128)(2,1)S(1)} reshape(bf16[1024,16,32]{2,1,0:T(8,128)(2,1)} %bitcast.114) | data formatting | bytes 2097152
  320.1 29.6 %all_to_all.76 = bf16[64,2,4096]{2,1,0:T(2,128)(2,1)S(1)} all-to-all(bf16[64,2,4096]{2,1,0:T(2,128)(2,1)S(1)} %reshape.214), channel_id=1, replica_groups=mesh['ta'=4,'pa'=64] {'pa'}, dimensions={0} | all-to-all | bytes 2097152 | tf_op jit(solution)/shard_map/all_to_all | solution.py:68
  349.7 3.5 reshape.215
  353.3 5.2 %copy.77 = bf16[32,16,1024]{2,1,0:T(8,128)(2,1)S(1)} copy(bf16[32,16,1024]{0,1,2:T(8,128)(2,1)} %bitcast.115) | data formatting | bytes 2097152 | tf_op jit(solution)/shard_map/all_to_all | solution.py:68
  358.5 4.2 copy.78
  362.7 7.8 %copy.79 = f32[32,64,16,16]{0,3,2,1:T(8,128)} copy(f32[32,64,16,16]{0,3,1,2:T(8,128)} %bitcast.111) | data formatting | bytes 4194304 | tf_op jit(solution)/shard_map/convert_element_type | solution.py:69
  370.6 6.8 %copy.80 = f32[32,1024,16]{1,2,0:T(8,128)} copy(f32[32,1024,16]{0,2,1:T(8,128)} %bitcast.109) | data formatting | bytes 4194304 | tf_op jit(solution)/shard_map/convert_element_type | solution.py:69
  377.4 5.2 %fusion.31 = bf16[32,4,256,16]{2,3,0,1:T(8,128)(2,1)S(1)} fusion(bf16[4,256,1024]{1,2,0:T(8,128)(2,1)S(1)} %copy-done.3, f32[2,32,4,1024,16]{3,4,1,0,2:T(8,128)} %copy-done.2, f32[32,1024,16]{1,2,0:T(8,128)} %copy.80), kind=kOutput, calls=%fused_computation.26 | convolution fusion | flops 1080557568 | bytes 13631488 | tf_op jit(solution)/shard_map/kip,tkpq->tkiq/dot_general | solution.py:70
  382.6 7.5 %copy.81 = bf16[32,4,256,16]{0,3,1,2:T(8,128)(2,1)} copy(bf16[32,4,256,16]{2,3,0,1:T(8,128)(2,1)S(1)} %fusion.31) | data formatting | bytes 2097152 | tf_op jit(solution)/shard_map/convert_element_type | solution.py:72
  390.1 7.3 %reshape.216 = bf16[64,2,4096]{2,1,0:T(2,128)(2,1)} reshape(bf16[256,4,16,32]{3,2,1,0:T(8,128)(2,1)} %bitcast.116) | data formatting | bytes 2097152
  397.3 6.5 %all-to-all-start.4 = ((bf16[64,2,4096]{2,1,0:T(2,128)(2,1)}), bf16[64,2,4096]{2,1,0:T(2,128)(2,1)S(1)}, u32[]{:S(2)}, u32[]{:S(2)}) async-start(bf16[64,2,4096]{2,1,0:T(2,128)(2,1)} %reshape.216), calls=%async_computation.4 | async-start | bytes 2097152 | tf_op jit(solution)/shard_map/all_to_all | solution.py:75
  403.8 21.3 %all-to-all-done.4 = bf16[64,2,4096]{2,1,0:T(2,128)(2,1)S(1)} async-done(((bf16[64,2,4096]{2,1,0:T(2,128)(2,1)}), bf16[64,2,4096]{2,1,0:T(2,128)(2,1)S(1)}, u32[]{:S(2)}, u32[]{:S(2)}) %all-to-all-start.4) | async-done | bytes 1048608 | tf_op jit(solution)/shard_map/all_to_all | solution.py:75
  425.1 3.5 reshape.217
  435.2 36.9 %all_to_all.77 = bf16[4,64,4,4,256]{4,1,3,2,0:T(8,128)(2,1)} all-to-all(bf16[4,64,4,4,256]{4,1,3,2,0:T(8,128)(2,1)S(1)} %copy.85), channel_id=1, replica_groups=mesh['ta'=4,'pa'=64] {'ta'}, dimensions={0} | all-to-all | bytes 4194304 | tf_op jit(solution)/shard_map/all_to_all | solution.py:18
  (25 shorter events, 25.6 us)
Async XLA Ops:
  6.5 235.6 %copy-start = (bf16[1024,1024]{1,0:T(8,128)(2,1)S(1)}, bf16[1024,1024]{1,0:T(8,128)(2,1)}, u32[]{:S(2)}) copy-start(bf16[1024,1024]{1,0:T(8,128)(2,1)} %param.5) | copy-start | bytes 6291460
  6.5 86.9 %all-gather.2.cloned.1.call-start = ((), (), s32[]{:S(2)}) async-start(), calls=%async_computation.6 | async-start | bytes 2129920 | tf_op jit(solution)/shard_map/all_gather | solution.py:46
  236.2 5.8 %copy-start.2 = (f32[2,32,4,1024,16]{3,4,1,0,2:T(8,128)}, f32[2,32,4,1024,16]{3,4,1,0,2:T(8,128)S(1)}, u32[]{:S(2)}) copy-start(f32[2,32,4,1024,16]{3,4,1,0,2:T(8,128)S(1)} %convolution_bitcast_fusion) | copy-start | bytes 50331652
  370.6 6.8 %copy-start.3 = (bf16[4,256,1024]{1,2,0:T(8,128)(2,1)S(1)}, bf16[4,256,1024]{1,2,0:T(8,128)(2,1)}, u32[]{:S(2)}) copy-start(bf16[4,256,1024]{1,2,0:T(8,128)(2,1)} %all-gather.2.cloned.1.call-done) | copy-start | bytes 6291460
  397.3 27.8 %all-to-all-start.4 = ((bf16[64,2,4096]{2,1,0:T(2,128)(2,1)}), bf16[64,2,4096]{2,1,0:T(2,128)(2,1)S(1)}, u32[]{:S(2)}, u32[]{:S(2)}) async-start(bf16[64,2,4096]{2,1,0:T(2,128)(2,1)} %reshape.216), calls=%async_computation.4 | async-start | bytes 2097152 | tf_op jit(solution)/shard_map/all_to_all | solution.py:75
  435.2 40.1 %copy-start.1 = (bf16[1024,1024]{1,0:T(8,128)(2,1)S(1)}, bf16[1024,1024]{1,0:T(8,128)(2,1)}, u32[]{:S(2)}) copy-start(bf16[1024,1024]{1,0:T(8,128)(2,1)} %param.5) | copy-start | bytes 6291460
Sparse Core Ops, SparseCore 0:
  10.5 82.9 all-gather.1
where the time goes:
time: 490 us; the launch traced here: 482 us
  blocking collectives  195 us (40%)
  local copies, waits for them, and re-layouts  166 us (34%)
  waiting for transfers between devices  70.7 us (14%)
  matrix products  23.1 us (5%)
  between operations  13.8 us (3%)
  other arithmetic  7.12 us (1%)
  starting transfers between devices  6.46 us (1%)
    all_to_all x2, blocking collectives, summed_on_arrival(): lax.all_to_all(blocks, axis, split_axis=0, concat_axis=0, tiled=True)  68.6 us
    unnamed x16, local copies, waits for them, and re-layouts  64 us
    all_to_all x1, blocking collectives, local(): lax.all_to_all(half_piece, 'pa', split_axis=4, concat_axis=3, tiled=True)  63.4 us
    all_gather x1, waiting for transfers between devices, local(): piece = lax.all_gather(colloc, 'pa', axis=2, tiled=True)  48.7 us
    all_to_all x1, blocking collectives, local(): lax.all_to_all(mixed, 'pa', split_axis=1, concat_axis=2, tiled=True)  33.4 us
    all_to_all x3, local copies, waits for them, and re-layouts, local(): lax.all_to_all(half_piece, 'pa', split_axis=4, concat_axis=3, tiled=True)  30.9 us
    all_to_all x1, blocking collectives, local(): lax.all_to_all(screened_rows, 'pa', split_axis=2, concat_axis=1, tiled=True)  29.6 us
    all_to_all x1, waiting for transfers between devices, local(): lax.all_to_all(outer, 'pa', split_axis=2, concat_axis=3, tiled=True)  21.3 us
  transfers between devices with their start and end apart: 2, of which 2 were waited for; matrix products, arithmetic and copies ran while one was open for 1% of the time, Pallas kernels for 0%

commit v1 on v0

--- a/solution.py
+++ b/solution.py
@@ -43,7 +43,9 @@
         "stw,wkij->stkij", fwd_part, green_freq.astype(jnp.float32), precision=lax.Precision.HIGHEST
     )
     green_time = summed_on_arrival(partial_time.astype(jnp.bfloat16), "ta", 1).astype(jnp.bfloat16)
-    piece = lax.all_gather(colloc, "pa", axis=2, tiled=True)
+    piece = jnp.concatenate(
+        lax.all_to_all(jnp.stack([colloc] * lax.axis_size("pa")), "pa", 0, 0), axis=2
+    )
     half_piece = jnp.einsum(
         "stkij,kjq->stkiq", green_time, piece, preferred_element_type=jnp.float32
     ).astype(jnp.bfloat16)

time: 490 us -> 481 us (0.982)
  blocking collectives: 195 us -> 180 us
  between operations: 13.8 us -> 0.65 us
  starting transfers between devices: 6.46 us -> 19.4 us
  local copies, waits for them, and re-layouts: 166 us -> 174 us
    all_to_all x0 -> x1, waiting for transfers between devices: none -> 50.2 us  [local(): lax.all_to_all(jnp.stack([colloc] * lax.axis_size('pa')), 'pa', 0, 0)]
    all_gather x1 -> x0, waiting for transfers between devices: 48.7 us -> none  [local(): piece = lax.all_gather(colloc, 'pa', axis=2, tiled=True)]
    all_to_all x0 -> x1, starting transfers between devices: none -> 12.8 us  [local(): lax.all_to_all(jnp.stack([colloc] * lax.axis_size('pa')), 'pa', 0, 0)]
    all_to_all x1, blocking collectives: 63.4 us -> 52.8 us  [local(): lax.all_to_all(half_piece, 'pa', split_axis=4, concat_axis=3, tiled=True)]
    unnamed x16 -> x18, local copies, waits for them, and re-layouts: 64 us -> 68.3 us
  transfers between devices with their start and end apart: 2 -> 2, of which waited for: 2 -> 2; matrix products, arithmetic and copies ran while one was open for 1% -> 0% of each run, Pallas kernels for 0% -> 0%
where the time goes in v1:
time: 481 us; the launch traced here: 472 us
  blocking collectives  180 us (37%)
  local copies, waits for them, and re-layouts  174 us (36%)
  waiting for transfers between devices  69.1 us (14%)
  matrix products  22.1 us (5%)
  starting transfers between devices  19.4 us (4%)
  other arithmetic  7.12 us (1%)
    all_to_all x2, blocking collectives, summed_on_arrival(): lax.all_to_all(blocks, axis, split_axis=0, concat_axis=0, tiled=True)  68.9 us
    unnamed x18, local copies, waits for them, and re-layouts  68.3 us
    all_to_all x1, blocking collectives, local(): lax.all_to_all(half_piece, 'pa', split_axis=4, concat_axis=3, tiled=True)  52.8 us
    all_to_all x1, waiting for transfers between devices, local(): lax.all_to_all(jnp.stack([colloc] * lax.axis_size('pa')), 'pa', 0, 0)  50.2 us
    all_to_all x1, blocking collectives, local(): lax.all_to_all(mixed, 'pa', split_axis=1, concat_axis=2, tiled=True)  30.9 us
    all_to_all x3, local copies, waits for them, and re-layouts, local(): lax.all_to_all(half_piece, 'pa', split_axis=4, concat_axis=3, tiled=True)  30.9 us
    all_to_all x1, blocking collectives, local(): lax.all_to_all(screened_rows, 'pa', split_axis=2, concat_axis=1, tiled=True)  27.5 us
    all_to_all x1, waiting for transfers between devices, local(): lax.all_to_all(outer, 'pa', split_axis=2, concat_axis=3, tiled=True)  19 us
  transfers between devices with their start and end apart: 2, of which 2 were waited for; matrix products, arithmetic and copies ran while one was open for 0% of the time, Pallas kernels for 0%

profile of v1, /device:TPU:1, one launch (start us, length us, event | category | flops | bytes accessed | tf_op | source)
XLA Modules:
  0.0 472.5 jit_solution(12471868017579000487)
XLA Ops:
  3.8 31.1 %all_to_all.78 = bf16[4,2,32,4,4,256]{5,2,4,3,1,0:T(8,128)(2,1)} all-to-all(bf16[4,2,32,4,4,256]{5,2,4,3,1,0:T(8,128)(2,1)S(1)} %bitcast.119), channel_id=1, replica_groups=mesh['ta'=4,'pa'=64] {'ta'}, dimensions={0} | all-to-all | bytes 4194304 | tf_op jit(solution)/shard_map/all_to_all | solution.py:18
  36.4 12.8 %all-to-all-start.1 = ((bf16[64,4,256,16]{2,3,1,0:T(8,128)(2,1)}), bf16[64,4,256,16]{2,3,1,0:T(8,128)(2,1)}, u32[]{:S(2)}, u32[]{:S(2)}) async-start(bf16[64,4,256,16]{2,3,1,0:T(8,128)(2,1)} %stack.5), calls=%async_computation.1 | async-start | bytes 4194304 | tf_op jit(solution)/shard_map/all_to_all | solution.py:47
  51.3 50.2 %all-to-all-done.1 = bf16[64,4,256,16]{2,3,1,0:T(8,128)(2,1)} async-done(((bf16[64,4,256,16]{2,3,1,0:T(8,128)(2,1)}), bf16[64,4,256,16]{2,3,1,0:T(8,128)(2,1)}, u32[]{:S(2)}, u32[]{:S(2)}) %all-to-all-start.1) | async-done | bytes 2097184 | tf_op jit(solution)/shard_map/all_to_all | solution.py:47
  106.6 13.3 %copy.85 = bf16[2,32,4,4,1024]{1,3,0,2,4:T(4,128)(2,1)} copy(bf16[2,32,4,4,1024]{4,1,3,0,2:T(8,128)(2,1)} %convert_bitcast_fusion) | data formatting | bytes 4194304 | tf_op jit(solution)/shard_map/convert_element_type | solution.py:51
  119.9 13.7 %reshape.219 = bf16[64,2,8192]{2,1,0:T(2,128)(2,1)} reshape(bf16[1024,4,2,4,32]{4,3,2,1,0:T(4,128)(2,1)} %bitcast.103) | data formatting | bytes 4194304
  133.6 52.8 %all_to_all.79 = bf16[64,2,8192]{2,1,0:T(2,128)(2,1)} all-to-all(bf16[64,2,8192]{2,1,0:T(2,128)(2,1)} %reshape.219), channel_id=1, replica_groups=mesh['ta'=4,'pa'=64] {'pa'}, dimensions={0} | all-to-all | bytes 4194304 | tf_op jit(solution)/shard_map/all_to_all | solution.py:58
  186.4 13.3 %reshape.220 = bf16[1024,4,2,4,32]{4,3,2,1,0:T(4,128)(2,1)} reshape(bf16[64,2,8192]{2,1,0:T(2,128)(2,1)} %all_to_all.79) | data formatting | bytes 4194304
  199.7 9.8 %copy.86 = bf16[2,32,4,4,1024]{1,4,3,2,0:T(8,128)(2,1)} copy(bf16[2,32,4,4,1024]{1,3,0,2,4:T(4,128)(2,1)} %bitcast.104) | data formatting | bytes 4194304 | tf_op jit(solution)/shard_map/all_to_all | solution.py:58
  209.5 9.1 %copy.87 = bf16[2,32,4,64,4,16]{1,5,4,3,2,0:T(8,128)(2,1)} copy(bf16[2,32,4,64,4,16]{1,5,3,4,2,0:T(8,128)(2,1)} %bitcast.107) | data formatting | bytes 4194304 | tf_op jit(solution)/shard_map/all_to_all | solution.py:58
  218.6 11.9 %copy.88 = bf16[2,32,4,256,16]{3,4,1,0,2:T(8,128)(2,1)} copy(bf16[2,32,4,256,16]{1,4,3,2,0:T(8,128)(2,1)} %bitcast.105) | data formatting | bytes 4194304 | tf_op jit(solution)/shard_map/all_to_all | solution.py:58
  230.5 4.6 convolution_bitcast_fusion
  242.3 5.1 %copy.90 = bf16[32,1024,16]{0,2,1:T(8,128)(2,1)} copy(bf16[32,1024,16]{1,2,0:T(8,128)(2,1)S(1)} %fusion.18) | data formatting | bytes 2097152 | tf_op jit(solution)/shard_map/convert_element_type | solution.py:65
  247.4 6.4 %reshape.221 = bf16[64,2,4096]{2,1,0:T(2,128)(2,1)S(1)} reshape(bf16[1024,16,32]{2,1,0:T(8,128)(2,1)} %bitcast.110) | data formatting | bytes 2097152
  253.9 30.9 %all_to_all.80 = bf16[64,2,4096]{2,1,0:T(2,128)(2,1)} all-to-all(bf16[64,2,4096]{2,1,0:T(2,128)(2,1)S(1)} %reshape.221), channel_id=1, replica_groups=mesh['ta'=4,'pa'=64] {'pa'}, dimensions={0} | all-to-all | bytes 2097152 | tf_op jit(solution)/shard_map/all_to_all | solution.py:66
  284.8 6.5 %reshape.222 = bf16[1024,16,32]{2,1,0:T(8,128)(2,1)} reshape(bf16[64,2,4096]{2,1,0:T(2,128)(2,1)} %all_to_all.80) | data formatting | bytes 2097152
  291.3 5.2 %copy.91 = bf16[32,16,64,16]{0,3,2,1:T(8,128)(2,1)} copy(bf16[32,16,64,16]{0,3,1,2:T(8,128)(2,1)} %bitcast.114) | data formatting | bytes 2097152 | tf_op jit(solution)/shard_map/all_to_all | solution.py:66
  296.6 4.0 copy.92
  302.7 7.4 %copy.93 = bf16[32,16,1024]{0,1,2:T(8,128)(2,1)} copy(bf16[32,16,1024]{2,1,0:T(8,128)(2,1)} %fusion.15) | data formatting | bytes 2097152 | tf_op jit(solution)/shard_map/convert_element_type | solution.py:69
  310.1 6.4 %reshape.223 = bf16[64,2,4096]{2,1,0:T(2,128)(2,1)S(1)} reshape(bf16[1024,16,32]{2,1,0:T(8,128)(2,1)} %bitcast.111) | data formatting | bytes 2097152
  316.6 27.5 %all_to_all.81 = bf16[64,2,4096]{2,1,0:T(2,128)(2,1)} all-to-all(bf16[64,2,4096]{2,1,0:T(2,128)(2,1)S(1)} %reshape.223), channel_id=1, replica_groups=mesh['ta'=4,'pa'=64] {'pa'}, dimensions={0} | all-to-all | bytes 2097152 | tf_op jit(solution)/shard_map/all_to_all | solution.py:70
  344.0 6.5 %reshape.224 = bf16[1024,16,32]{2,1,0:T(8,128)(2,1)} reshape(bf16[64,2,4096]{2,1,0:T(2,128)(2,1)} %all_to_all.81) | data formatting | bytes 2097152
  350.6 5.2 %copy.94 = bf16[32,16,1024]{2,1,0:T(8,128)(2,1)S(1)} copy(bf16[32,16,1024]{0,1,2:T(8,128)(2,1)} %bitcast.112) | data formatting | bytes 2097152 | tf_op jit(solution)/shard_map/all_to_all | solution.py:70
  355.8 4.2 copy.95
  360.1 7.8 %copy.96 = f32[32,64,16,16]{0,3,2,1:T(8,128)} copy(f32[32,64,16,16]{0,3,1,2:T(8,128)} %bitcast.108) | data formatting | bytes 4194304 | tf_op jit(solution)/shard_map/convert_element_type | solution.py:71
  367.9 6.6 %copy.97 = f32[32,1024,16]{1,2,0:T(8,128)} copy(f32[32,1024,16]{0,2,1:T(8,128)} %bitcast.106) | data formatting | bytes 4194304 | tf_op jit(solution)/shard_map/convert_element_type | solution.py:71
  374.5 5.8 %fusion.21 = bf16[32,4,256,16]{2,3,0,1:T(8,128)(2,1)S(1)} fusion(bf16[4,256,1024,1]{1,2,3,0:T(8,128)(2,1)} %bitcast.101, f32[2,32,4,1024,16]{3,4,1,0,2:T(8,128)} %copy-done.1, f32[32,1024,16]{1,2,0:T(8,128)} %copy.97), kind=kOutput, calls=%fused_computation.20 | convolution fusion | flops 1080557568 | bytes 13631488 | tf_op jit(solution)/shard_map/kip,tkpq->tkiq/dot_general | solution.py:72
  380.3 7.5 %copy.99 = bf16[32,4,256,16]{0,3,1,2:T(8,128)(2,1)} copy(bf16[32,4,256,16]{2,3,0,1:T(8,128)(2,1)S(1)} %fusion.21) | data formatting | bytes 2097152 | tf_op jit(solution)/shard_map/convert_element_type | solution.py:74
  387.8 7.3 %reshape.225 = bf16[64,2,4096]{2,1,0:T(2,128)(2,1)} reshape(bf16[256,4,16,32]{3,2,1,0:T(8,128)(2,1)} %bitcast.113) | data formatting | bytes 2097152
  395.1 6.6 %all-to-all-start.5 = ((bf16[64,2,4096]{2,1,0:T(2,128)(2,1)}), bf16[64,2,4096]{2,1,0:T(2,128)(2,1)S(1)}, u32[]{:S(2)}, u32[]{:S(2)}) async-start(bf16[64,2,4096]{2,1,0:T(2,128)(2,1)} %reshape.225), calls=%async_computation.5 | async-start | bytes 2097152 | tf_op jit(solution)/shard_map/all_to_all | solution.py:77
  401.6 19.0 %all-to-all-done.5 = bf16[64,2,4096]{2,1,0:T(2,128)(2,1)S(1)} async-done(((bf16[64,2,4096]{2,1,0:T(2,128)(2,1)}), bf16[64,2,4096]{2,1,0:T(2,128)(2,1)S(1)}, u32[]{:S(2)}, u32[]{:S(2)}) %all-to-all-start.5) | async-done | bytes 1048608 | tf_op jit(solution)/shard_map/all_to_all | solution.py:77
  420.6 3.5 reshape.226
  431.0 37.9 %all_to_all.82 = bf16[4,64,4,4,256]{4,1,3,2,0:T(8,128)(2,1)} all-to-all(bf16[4,64,4,4,256]{4,1,3,2,0:T(8,128)(2,1)S(1)} %copy.104), channel_id=1, replica_groups=mesh['ta'=4,'pa'=64] {'ta'}, dimensions={0} | all-to-all | bytes 4194304 | tf_op jit(solution)/shard_map/all_to_all | solution.py:18
  (28 shorter events, 31.9 us)
Async XLA Ops:
  0.0 241.0 %copy-start = (bf16[1024,1024]{1,0:T(8,128)(2,1)S(1)}, bf16[1024,1024]{1,0:T(8,128)(2,1)}, u32[]{:S(2)}) copy-start(bf16[1024,1024]{1,0:T(8,128)(2,1)} %param.5) | copy-start | bytes 6291460
  3.8 31.1 %copy-start.4 = (bf16[4,256,16]{1,2,0:T(8,128)(2,1)S(1)}, bf16[4,256,16]{1,2,0:T(8,128)(2,1)}, u32[]{:S(2)}) copy-start(bf16[4,256,16]{1,2,0:T(8,128)(2,1)} %param.4) | copy-start | bytes 98308
  36.4 65.0 %all-to-all-start.1 = ((bf16[64,4,256,16]{2,3,1,0:T(8,128)(2,1)}), bf16[64,4,256,16]{2,3,1,0:T(8,128)(2,1)}, u32[]{:S(2)}, u32[]{:S(2)}) async-start(bf16[64,4,256,16]{2,3,1,0:T(8,128)(2,1)} %stack.5), calls=%async_computation.1 | async-start | bytes 4194304 | tf_op jit(solution)/shard_map/all_to_all | solution.py:47
  103.2 1.3 copy-start.2
  235.2 5.8 %copy-start.1 = (f32[2,32,4,1024,16]{3,4,1,0,2:T(8,128)}, f32[2,32,4,1024,16]{3,4,1,0,2:T(8,128)S(1)}, u32[]{:S(2)}) copy-start(f32[2,32,4,1024,16]{3,4,1,0,2:T(8,128)S(1)} %convolution_bitcast_fusion) | copy-start | bytes 50331652
  395.1 25.6 %all-to-all-start.5 = ((bf16[64,2,4096]{2,1,0:T(2,128)(2,1)}), bf16[64,2,4096]{2,1,0:T(2,128)(2,1)S(1)}, u32[]{:S(2)}, u32[]{:S(2)}) async-start(bf16[64,2,4096]{2,1,0:T(2,128)(2,1)} %reshape.225), calls=%async_computation.5 | async-start | bytes 2097152 | tf_op jit(solution)/shard_map/all_to_all | solution.py:77
  424.1 3.4 copy-start.3
